TPU v7x, 32 devices: a whole 2x2x4 slice. The times are simulated.
32 devices in a mesh: groups: 2 (over y), tm: 4 (over z), dp: 2 (over x), head: 2 (over core).
Axes of the slice: x: 2, y: 2, z: 4, core: 2. Of those that a mesh axis runs over, the one named last changes fastest.
Arguments:
- frames: bfloat16 [4, 7168, 512], P(('groups', 'dp'), 'tm', 'head'), parts along dimension 0, may hold values from -8 to 8
- lengths: int32 [4], P(('groups', 'dp')), parts along dimension 0, may hold values from 1792 to 7168, as said below
- down_weights: float32 [4, 512], P(None, 'head'), may hold values from 0.1 to 0.4
- w_query: bfloat16 [512, 256], P(None, 'head'), may hold values from -0.79549513 to 0.79549513
- w_key: bfloat16 [512, 256], P(None, 'head'), may hold values from -0.79549513 to 0.79549513
- w_value: bfloat16 [512, 96], P(None, 'head'), may hold values from -0.25 to 0.25
- w_out: bfloat16 [96, 512], P('head'), may hold values from -0.625 to 0.625
- conv_in: bfloat16 [512, 2, 512], P(None, None, 'head'), may hold values from -0.25 to 0.25
- conv_taps: float32 [31, 512], P(None, 'head'), may hold values from -1.8 to 1.8
- conv_out: bfloat16 [512, 512], P('head'), may hold values from -0.25 to 0.25
- bypass: float32 [512], P('head'), may hold values from 0.2 to 0.9
Outputs:
- stack_out: bfloat16 [4, 7168, 512], P(('groups', 'dp'), 'tm', 'head'), parts along dimension 0
There are 2 independent parts, one for each index of `groups`. A program takes and returns all parts, laid end to end along the dimension named above; an argument that names none is the same for every part. Nothing has to cross between parts.
Inputs may be any that keep to these rules, and one draw needn't show every extreme that they name: `lengths`: valid frames of each recording; the later slots are padding. In every part some recording has all 7168 frames.
All inputs are finite; a program needn't handle non-finite values.
Results may differ from a plain program's by a relative error of at most 0.009.
Values may be sent and summed in bfloat16 or wider, within the bound.
No kernel may reach another device: no remote copies, remote signals or barrier semaphores. Data moves between devices by JAX's collectives and lax.ppermute only.
A program may use at most 64 MiB of HBM per device.

v0:
```python
import jax
import jax.numpy as jnp
from jax import lax
from jax.sharding import PartitionSpec as P

QDIM = 32
VDIM = 12


def with_halo(block, sides, width):
    for axis, dim in sides:
        count = lax.axis_size(axis)
        forward = [(i, i + 1) for i in range(count - 1)]
        backward = [(target, source) for source, target in forward]
        low = lax.ppermute(
            lax.slice_in_dim(block, block.shape[dim] - width, None, axis=dim), axis, forward
        )
        high = lax.ppermute(lax.slice_in_dim(block, 0, width, axis=dim), axis, backward)
        block = jnp.concatenate([low, block, high], axis=dim)
    return block


def shards(
    frames,
    lengths,
    down_weights,
    w_query,
    w_key,
    w_value,
    w_out,
    conv_in,
    conv_taps,
    conv_out,
    bypass,
):
    records, frame_count, channels = frames.shape
    quarter = frame_count // 4
    group_size = lax.axis_size("tm")
    group_index = lax.axis_index("tm")
    positions = group_index * frame_count + jnp.arange(frame_count)
    frame_live = positions[None, :] < lengths[:, None]
    masked = jnp.where(frame_live[:, :, None], frames, jnp.zeros_like(frames))
    grouped = masked.reshape(records, quarter, 4, channels).astype(jnp.float32)
    reduced = jnp.sum(grouped * down_weights[None, None], axis=2).astype(jnp.bfloat16)
    live_rows = (lengths + 3) // 4
    row_index = group_index * quarter + jnp.arange(quarter)
    row_live = row_index[None, :] < live_rows[:, None]
    full_rows = lax.all_gather(reduced, "head", axis=2, tiled=True)
    heads_here = w_query.shape[1] // QDIM
    queries = jnp.einsum("rsd,dk->rsk", full_rows, w_query, preferred_element_type=jnp.float32)
    queries = queries.astype(jnp.bfloat16).reshape(records, quarter, heads_here, QDIM)
    segment = lax.all_gather(full_rows, "tm", axis=1, tiled=True)
    keys_t = jnp.einsum("rnd,dk->rkn", segment, w_key, preferred_element_type=jnp.float32)
    values_t = jnp.einsum("rnd,dk->rkn", segment, w_value, preferred_element_type=jnp.float32)
    packed = jnp.concatenate([keys_t, values_t], axis=1).astype(jnp.bfloat16)
    key_width = heads_here * QDIM
    key_block = 2 * quarter
    block_count = group_size // 2
    score_scale = QDIM ** (-0.5)
    key_offsets = jnp.arange(key_block)
    initial = (
        jnp.full((records, heads_here, quarter), -1e30, jnp.float32),
        jnp.zeros((records, heads_here, quarter), jnp.float32),
        jnp.zeros((records, heads_here, quarter, VDIM), jnp.float32),
    )

    def merge_block(query_set, segment, key_live, running):
        top_score, denominator, weighted = running
        count_rows = segment.shape[0]
        key_rows = segment[:, :key_width].reshape(count_rows, heads_here, QDIM, key_block)
        value_rows = segment[:, key_width:].reshape(count_rows, heads_here, VDIM, key_block)
        scores = (
            jnp.einsum("rqhd,rhdk->rhqk", query_set, key_rows, preferred_element_type=jnp.float32)
            * score_scale
        )
        scores = jnp.where(key_live[:, None, None, :], scores, jnp.float32(-1e30))
        new_top = jnp.maximum(top_score, jnp.max(scores, axis=-1))
        factor = jnp.exp(top_score - new_top)
        expo = jnp.where(
            key_live[:, None, None, :], jnp.exp(scores - new_top[..., None]), jnp.float32(0.0)
        )
        denominator = denominator * factor + jnp.sum(expo, axis=-1)
        weighted = weighted * factor[..., None] + jnp.einsum(
            "rhqk,rhvk->rhqv",
            expo.astype(jnp.bfloat16),
            value_rows,
            preferred_element_type=jnp.float32,
        )
        return (new_top, denominator, weighted)

    def advance_all(block_index, running):
        first_key = block_index * key_block
        segment = lax.dynamic_slice_in_dim(packed, first_key, key_block, 2)
        key_live = (first_key + key_offsets)[None, :] < live_rows[:, None]
        return merge_block(queries, segment, key_live, running)

    top_score, denominator, weighted = lax.fori_loop(0, block_count, advance_all, initial)
    attended = weighted / denominator[..., None]
    attended = (
        jnp.transpose(attended, (0, 2, 1, 3))
        .reshape(records, quarter, heads_here * VDIM)
        .astype(jnp.bfloat16)
    )
    partial_value = jnp.einsum("rsv,vd->rsd", attended, w_out, preferred_element_type=jnp.float32)
    attn_half = lax.psum_scatter(
        partial_value.astype(jnp.bfloat16), "head", scatter_dimension=2, tiled=True
    ).astype(jnp.float32)
    after_attn = (reduced.astype(jnp.float32) + attn_half).astype(jnp.bfloat16)
    attn_rows = lax.all_gather(after_attn, "head", axis=2, tiled=True)
    gates = jnp.einsum("rsd,dgc->rsgc", attn_rows, conv_in, preferred_element_type=jnp.float32)
    gated = gates[:, :, 0] * jax.nn.sigmoid(gates[:, :, 1])
    gated = jnp.where(row_live[:, :, None], gated, jnp.float32(0.0)).astype(jnp.bfloat16)
    reach = conv_taps.shape[0] // 2
    padded = with_halo(gated, (("tm", 1),), reach)
    depthwise = jnp.zeros((records, quarter, channels), jnp.float32)
    for tap_index in range(conv_taps.shape[0]):
        depthwise = depthwise + conv_taps[tap_index][None, None, :] * padded[
            :, tap_index : tap_index + quarter
        ].astype(jnp.float32)
    hidden = jax.nn.silu(depthwise).astype(jnp.bfloat16)
    conv_part = jnp.einsum("rsc,cd->rsd", hidden, conv_out, preferred_element_type=jnp.float32)
    conv_half = lax.psum_scatter(
        conv_part.astype(jnp.bfloat16), "head", scatter_dimension=2, tiled=True
    ).astype(jnp.float32)
    stacked = after_attn.astype(jnp.float32) + conv_half
    upsampled = jnp.repeat(stacked, 4, axis=1)
    backdrop = frames.astype(jnp.float32)
    result = backdrop + bypass[None, None, :] * (upsampled - backdrop)
    return jnp.where(frame_live[:, :, None], result, jnp.float32(0.0)).astype(jnp.bfloat16)


def solution(mesh):
    in_specs = (
        P(("groups", "dp"), "tm", "head"),
        P(("groups", "dp")),
        P(None, "head"),
        P(None, "head"),
        P(None, "head"),
        P(None, "head"),
        P("head", None),
        P(None, None, "head"),
        P(None, "head"),
        P("head", None),
        P("head"),
    )
    out_specs = P(("groups", "dp"), "tm", "head")
    return jax.shard_map(shards, mesh=mesh, in_specs=in_specs, out_specs=out_specs, check_vma=False)
```

profile of v0, /device:TPU:0, one launch (start us, length us, event | category | flops | bytes accessed | tf_op | source)
XLA Modules:
  0.0 135.5 jit_solution(3686259870509432775)
XLA Ops:
  6.5 0.0 copy-start
  6.5 0.0 all-gather.4.cloned.1.call-start
  7.3 0.0 copy-start.8
  7.3 0.6 copy-done.8
  7.9 2.7 %select_convert_fusion = f32[1,1792,256]{2,1,0:T(8,128)} fusion(bf16[1,1792,256]{2,1,0:T(8,128)(2,1)} %param.13, pred[1792]{0:T(1024)(128)(4,1)S(1)} %add_compare_fusion), kind=kLoop, calls=%fused_computation.72 | loop fusion | flops 917504 | bytes 2754304 | tf_op jit(solution)/shard_map/convert_element_type | solution.py:43
  10.6 1.8 %reshape.448 = f32[1,448,4,256]{3,2,1,0:T(4,128)S(1)} reshape(f32[1,1792,256]{2,1,0:T(8,128)} %select_convert_fusion) | data formatting | bytes 3670016 | tf_op jit(solution)/shard_map/convert_element_type | solution.py:43
  12.4 0.0 copy-done.10
  12.5 0.0 copy-start.5
  12.5 0.0 copy-start.4
  12.5 1.3 multiply_reduce_fusion
  13.8 0.0 copy-start.3
  13.8 0.7 copy-done.3
  14.5 2.4 %all-gather = bf16[448,512]{1,0:T(8,128)(2,1)} all-gather(bf16[448,256]{1,0:T(8,128)(2,1)S(1)} %multiply_reduce_fusion), channel_id=2, replica_groups=mesh['groups'=2,'tm'=4,'dp'=2,'head'=2] {'head'}, dimensions={1}, use_global_device_ids=true | all-gather | bytes 688128 | tf_op jit(solution)/shard_map/all_gather | solution.py:48
  16.9 0.0 all-gather.4.cloned.1.call-update
  16.9 0.0 reduce-scatter.3.cloned.1.call-start
  17.0 0.0 copy-done.5
  17.0 1.3 convolution_convert_fusion.4
  18.3 0.8 copy.14
  19.1 41.9 %all-gather.4.cloned.1.call-done = bf16[1792,512]{1,0:T(8,128)(2,1)} async-done(((bf16[448,512]{1,0:T(8,128)(2,1)}), bf16[1792,512]{1,0:T(8,128)(2,1)}) %all-gather.4.cloned.1.call-update) | async-done | bytes 1835024 | tf_op jit(solution)/shard_map/all_gather | solution.py:52
  61.0 0.0 copy-done.4
  61.0 2.4 %fusion.23 = bf16[1,128,1792]{2,1,0:T(8,128)(2,1)S(1)} fusion(bf16[1792,512]{1,0:T(8,128)(2,1)} %all-gather.4.cloned.1.call-done, bf16[512,128]{1,0:T(8,128)(2,1)S(1)} %copy-done.4), kind=kOutput, calls=%fused_computation.29 | convolution fusion | flops 235110400 | bytes 2424832 | tf_op jit(solution)/shard_map/rnd,dk->rkn/dot_general | solution.py:53
  63.3 0.0 copy-done.7
  63.4 0.0 copy-done.1
  63.4 0.6 fusion.24
  64.1 0.0 copy-start.6
  64.1 25.0 %while.18 = (s32[]{:T(128)}, f32[1,4,448]{2,1,0:T(4,128)S(1)}, f32[1,4,448]{2,1,0:T(4,128)S(1)}, f32[1,4,448,12]{2,3,1,0:T(8,128)}, s32[1]{0:T(128)}, /*index=5*...) while((s32[]{:T(128)}, f32[1,4,448]{2,1,0:T(4,128)S(1)}, ...), condition=%wide.region_4.5_spmd.clone, body=%wide.region_1.4_spmd.clone.sunk | while | flops 162245888 | bytes 40058620 | solution.py:97
  64.1 4.8 %bitcast_reduce_fusion.2 = (f32[4,448]{1,0:T(4,128)S(1)}, f32[4,896,448]{1,2,0:T(8,128)}) fusion(pred[896]{0:T(1024)(128)(4,1)S(1)} %fusion.96, bf16[4,32,896]{2,1,0:T(8,128)(2,1)S(1)} %bitcast.144, bf16[1,448,4,32]{1,3,2,0:T(8,128)(2,1)} %get-tuple-element.312), kind=kOutput, calls=%fused_computation.2.clone.1 | convolution fusion | flops 107575552 | bytes 6774656 | tf_op jit(solution)/shard_map/while/body/eval_jaxpr/rqhd,rhdk->rhqk/dot_general | solution.py:73
  69.0 0.0 slice-start
  69.0 0.7 reshape.460
  69.7 5.0 %fusion.99 = f32[1,4,448,12]{2,3,1,0:T(8,128)} fusion(bf16[4,12,896]{2,1,0:T(8,128)(2,1)} %reshape.460, f32[4,896,448]{1,2,0:T(8,128)} %get-tuple-element.280, f32[4,448]{1,0:T(4,128)S(1)} %bitcast.145, pred[896]{0:T(1024)(128)(4,1)S(1)} %fusion.96, f32[1,4,448,12]{2,3,1,0:T(8,128)} %get-tuple-element.297, f32[4,448]{1,0:T(4,128)S(1)} %get-tuple-element.281, ...), kind=kOutput, calls=%fused_computation.12.clone.1 | convolution fusion | flops 46627840 | bytes 6695809 | tf_op jit(solution)/shard_map/while/body/eval_jaxpr/rhqk,rhvk->rhqv/dot_general | solution.py:83
  74.7 0.0 slice-done
  74.7 0.0 slice-done.1
  74.7 1.8 %fusion.98 = f32[4,448]{1,0:T(4,128)S(1)} fusion(f32[4,896,448]{1,2,0:T(8,128)S(1)} %bitcast.143, f32[4,448]{1,0:T(4,128)S(1)} %bitcast.146, pred[896]{0:T(1024)(128)(4,1)S(1)} %fusion.96), kind=kLoop, calls=%fused_computation.7.clone.1 | loop fusion | flops 8026368 | bytes 6437760 | tf_op jit(solution)/shard_map/while/body/eval_jaxpr/reduce_sum | solution.py:82
  76.6 4.8 %bitcast_reduce_fusion.2 = (f32[4,448]{1,0:T(4,128)S(1)}, f32[4,896,448]{1,2,0:T(8,128)}) fusion(pred[896]{0:T(1024)(128)(4,1)S(1)} %fusion.96, bf16[4,32,896]{2,1,0:T(8,128)(2,1)S(1)} %bitcast.144, bf16[1,448,4,32]{1,3,2,0:T(8,128)(2,1)} %get-tuple-element.312), kind=kOutput, calls=%fused_computation.2.clone.1 | convolution fusion | flops 107575552 | bytes 6774656 | tf_op jit(solution)/shard_map/while/body/eval_jaxpr/rqhd,rhdk->rhqk/dot_general | solution.py:73
  81.5 0.0 slice-start
  81.5 0.7 reshape.460
  82.1 5.0 %fusion.99 = f32[1,4,448,12]{2,3,1,0:T(8,128)} fusion(bf16[4,12,896]{2,1,0:T(8,128)(2,1)} %reshape.460, f32[4,896,448]{1,2,0:T(8,128)} %get-tuple-element.280, f32[4,448]{1,0:T(4,128)S(1)} %bitcast.145, pred[896]{0:T(1024)(128)(4,1)S(1)} %fusion.96, f32[1,4,448,12]{2,3,1,0:T(8,128)} %get-tuple-element.297, f32[4,448]{1,0:T(4,128)S(1)} %get-tuple-element.281, ...), kind=kOutput, calls=%fused_computation.12.clone.1 | convolution fusion | flops 46627840 | bytes 6695809 | tf_op jit(solution)/shard_map/while/body/eval_jaxpr/rhqk,rhvk->rhqv/dot_general | solution.py:83
  87.2 0.0 slice-done
  87.2 0.0 slice-done.1
  87.2 1.8 %fusion.98 = f32[4,448]{1,0:T(4,128)S(1)} fusion(f32[4,896,448]{1,2,0:T(8,128)S(1)} %bitcast.143, f32[4,448]{1,0:T(4,128)S(1)} %bitcast.146, pred[896]{0:T(1024)(128)(4,1)S(1)} %fusion.96), kind=kLoop, calls=%fused_computation.7.clone.1 | loop fusion | flops 8026368 | bytes 6437760 | tf_op jit(solution)/shard_map/while/body/eval_jaxpr/reduce_sum | solution.py:82
  89.0 0.9 fusion.69
  90.0 0.0 copy-done.6
  90.0 1.1 fusion.28
  91.1 0.0 reduce-scatter.3.cloned.1.call-update
  91.1 0.0 reduce-scatter.5.cloned.1.call-start
  91.2 1.0 fusion.73
  92.2 5.8 %reduce-scatter.3.cloned.1.call-done = bf16[1,448,256]{2,1,0:T(8,128)(2,1)} async-done(((bf16[1,448,512]{2,1,0:T(8,128)(2,1)}), bf16[1,448,256]{2,1,0:T(8,128)(2,1)}) %reduce-scatter.3.cloned.1.call-update) | async-done | bytes 229392 | tf_op jit(solution)/shard_map/reduce_scatter | solution.py:105
  98.0 1.1 fusion.37
  99.1 0.0 copy-start.12
  99.1 2.3 %all_gather.11 = bf16[1,448,512]{2,1,0:T(8,128)(2,1)S(1)} all-gather(bf16[1,448,256]{2,1,0:T(8,128)(2,1)S(1)} %fusion.37), channel_id=1, replica_groups=mesh['groups'=2,'tm'=4,'dp'=2,'head'=2] {'head'}, dimensions={2}, use_global_device_ids=true | all-gather | bytes 688128 | tf_op jit(solution)/shard_map/all_gather | solution.py:109
  101.3 0.4 convolution_bitcast_fusion
  101.8 0.2 fusion.39
  101.9 3.6 %collective-permute-start = (bf16[1,15,256]{2,1,0:T(8,128)(2,1)S(1)}, bf16[1,15,256]{2,1,0:T(8,128)(2,1)S(1)}, u32[]{:S(2)}, u32[]{:S(2)}) collective-permute-start(bf16[1,15,256]{2,1,0:T(8,128)(2,1)S(1)} %get-tuple-element.198), channel_id=1, source_target_pairs={{0,4},{4,8},{8,12},{1,5},{5,9},{9,13},{2,6},{6,10},{10,14},{3,7},{... | collective-permute-start | bytes 23048 | tf_op jit(solution)/shard_map/ppermute | solution.py:15
  105.5 1.3 collective-permute-start.1
  106.8 1.0 fusion.74
  107.8 0.0 collective-permute-done
  107.8 3.3 %collective-permute-done.1 = bf16[1,15,256]{2,1,0:T(8,128)(2,1)S(1)} collective-permute-done((bf16[1,15,256]{2,1,0:T(8,128)(2,1)S(1)}, bf16[1,15,256]{2,1,0:T(8,128)(2,1)S(1)}, u32[]{:S(2)}, u32[]{:S(2)}) %collective-permute-start.1) | collective-permute-done | bytes 7712 | tf_op jit(solution)/shard_map/ppermute | solution.py:18
  111.1 4.0 %fusion.29 = bf16[1,448,512]{2,1,0:T(8,128)(2,1)} fusion(bf16[256,512]{1,0:T(8,128)(2,1)S(1)} %copy-done.12, bf16[1,448,256]{2,1,0:T(8,128)(2,1)S(1)} %fusion.39, bf16[1,15,256]{2,1,0:T(8,128)(2,1)S(1)} %collective-permute-done.1, bf16[1,15,256]{2,1,0:T(8,128)(2,1)S(1)} %collective-permute-done, f32[256]{0:T(256)S(1)} %bitcast.177, f32[256]{0:T(256)S(1)} %bitcast.178, ...), kind=kOutput, calls=%fused_computation.70 | convolution fusion | flops 139116544 | bytes 997376 | tf_op jit(solution)/shard_map/rsc,cd->rsd/dot_general | solution.py:121
  115.0 0.0 reduce-scatter.5.cloned.1.call-update
  115.1 8.0 %reduce-scatter.5.cloned.1.call-done = bf16[1,448,256]{2,1,0:T(8,128)(2,1)} async-done(((bf16[1,448,512]{2,1,0:T(8,128)(2,1)}), bf16[1,448,256]{2,1,0:T(8,128)(2,1)}) %reduce-scatter.5.cloned.1.call-update) | async-done | bytes 229392 | tf_op jit(solution)/shard_map/reduce_scatter | solution.py:122
  123.1 1.0 add_bitcast_fusion
  124.1 1.6 %broadcast_in_dim.110 = f32[448,4,256]{2,1,0:T(4,128)} broadcast(f32[448,256]{1,0:T(8,128)S(1)} %add_bitcast_fusion), dimensions={0,2} | broadcast | bytes 2293760 | tf_op jit(solution)/shard_map/broadcast_in_dim | solution.py:126
  125.7 2.0 %broadcast_in_dim.111 = f32[1,1792,256]{2,1,0:T(8,128)S(1)} reshape(f32[448,4,256]{2,1,0:T(4,128)} %broadcast_in_dim.110) | data formatting | bytes 3670016 | tf_op jit(solution)/shard_map/broadcast_in_dim | solution.py:126
  127.7 1.3 fusion.27
  (35 shorter events, 0.3 us)
Async XLA Ops:
  6.5 94.8 %copy-start = (bf16[512,2,256]{2,1,0:T(2,128)(2,1)S(1)}, bf16[512,2,256]{2,1,0:T(2,128)(2,1)}, u32[]{:S(2)}) copy-start(bf16[512,2,256]{2,1,0:T(2,128)(2,1)} %param.20) | copy-start | bytes 1572868
  6.5 54.4 %all-gather.4.cloned.1.call-start = ((), (), s32[]{:S(2)}) async-start(), calls=%async_computation.4 | async-start | bytes 2293760 | tf_op jit(solution)/shard_map/all_gather | solution.py:52
  7.3 0.6 copy-start.8
  10.6 1.9 %copy-start.10 = (f32[4,256]{1,0:T(4,128)S(1)}, f32[4,256]{1,0:T(4,128)}, u32[]{:S(2)}) copy-start(f32[4,256]{1,0:T(4,128)} %param.15) | copy-start | bytes 12292
  12.5 4.5 %copy-start.5 = (bf16[512,128]{1,0:T(8,128)(2,1)S(1)}, bf16[512,128]{1,0:T(8,128)(2,1)}, u32[]{:S(2)}) copy-start(bf16[512,128]{1,0:T(8,128)(2,1)} %param.16) | copy-start | bytes 393220
  12.5 48.5 %copy-start.4 = (bf16[512,128]{1,0:T(8,128)(2,1)S(1)}, bf16[512,128]{1,0:T(8,128)(2,1)}, u32[]{:S(2)}) copy-start(bf16[512,128]{1,0:T(8,128)(2,1)} %param.17) | copy-start | bytes 393220
  13.8 0.7 copy-start.3
  16.9 46.5 %copy-start.7 = (bf16[512,48]{0,1:T(8,128)(2,1)S(1)}, bf16[512,48]{0,1:T(8,128)(2,1)}, u32[]{:S(2)}) copy-start(bf16[512,48]{0,1:T(8,128)(2,1)} %param.18) | copy-start | bytes 147460
  16.9 81.1 %reduce-scatter.3.cloned.1.call-start = ((), (), s32[]{:S(2)}) async-start(), calls=%async_computation.2 | async-start | bytes 688128 | tf_op jit(solution)/shard_map/reduce_scatter | solution.py:105
  61.0 2.4 %copy-start.1 = (bf16[1792,512]{1,0:T(8,128)(2,1)S(1)}, bf16[1792,512]{1,0:T(8,128)(2,1)}, u32[]{:S(2)}) copy-start(bf16[1792,512]{1,0:T(8,128)(2,1)} %all-gather.4.cloned.1.call-done) | copy-start | bytes 5505028
  64.1 25.9 %copy-start.6 = (bf16[48,512]{1,0:T(8,128)(2,1)S(1)}, bf16[48,512]{1,0:T(8,128)(2,1)}, u32[]{:S(2)}) copy-start(bf16[48,512]{1,0:T(8,128)(2,1)} %param.19) | copy-start | bytes 147460
  69.0 5.7 %slice-start = ((s8[6422528]{0:T(1024)(128)(4,1)}), s8[2228224]{0:T(1024)(128)(4,1)S(1)}, s32[]{:S(2)}) async-start(s8[6422528]{0:T(1024)(128)(4,1)} %bitcast.142), calls=%async_computation.5 | async-start | bytes 4456448 | tf_op jit(solution)/shard_map/while
  69.7 5.0 %slice-start.1 = ((s8[6422528]{0:T(1024)(128)(4,1)}), s8[4194304]{0:T(1024)(128)(4,1)S(1)}, s32[]{:S(2)}) async-start(s8[6422528]{0:T(1024)(128)(4,1)} %bitcast.142), calls=%async_computation.6 | async-start | bytes 8388608 | tf_op jit(solution)/shard_map/while
  81.5 5.7 %slice-start = ((s8[6422528]{0:T(1024)(128)(4,1)}), s8[2228224]{0:T(1024)(128)(4,1)S(1)}, s32[]{:S(2)}) async-start(s8[6422528]{0:T(1024)(128)(4,1)} %bitcast.142), calls=%async_computation.5 | async-start | bytes 4456448 | tf_op jit(solution)/shard_map/while
  82.1 5.0 %slice-start.1 = ((s8[6422528]{0:T(1024)(128)(4,1)}), s8[4194304]{0:T(1024)(128)(4,1)S(1)}, s32[]{:S(2)}) async-start(s8[6422528]{0:T(1024)(128)(4,1)} %bitcast.142), calls=%async_computation.6 | async-start | bytes 8388608 | tf_op jit(solution)/shard_map/while
  91.1 32.0 %reduce-scatter.5.cloned.1.call-start = ((), (), s32[]{:S(2)}) async-start(), calls=%async_computation.3 | async-start | bytes 688128 | tf_op jit(solution)/shard_map/reduce_scatter | solution.py:122
  99.1 12.0 %copy-start.12 = (bf16[256,512]{1,0:T(8,128)(2,1)S(1)}, bf16[256,512]{1,0:T(8,128)(2,1)}, u32[]{:S(2)}) copy-start(bf16[256,512]{1,0:T(8,128)(2,1)} %param.22) | copy-start | bytes 786436
  101.9 5.9 %collective-permute-start = (bf16[1,15,256]{2,1,0:T(8,128)(2,1)S(1)}, bf16[1,15,256]{2,1,0:T(8,128)(2,1)S(1)}, u32[]{:S(2)}, u32[]{:S(2)}) collective-permute-start(bf16[1,15,256]{2,1,0:T(8,128)(2,1)S(1)} %get-tuple-element.198), channel_id=1, source_target_pairs={{0,4},{4,8},{8,12},{1,5},{5,9},{9,13},{2,6},{6,10},{10,14},{3,7},{... | collective-permute-start | bytes 23048 | tf_op jit(solution)/shard_map/ppermute | solution.py:15
  105.5 5.5 %collective-permute-start.1 = (bf16[1,15,256]{2,1,0:T(8,128)(2,1)S(1)}, bf16[1,15,256]{2,1,0:T(8,128)(2,1)S(1)}, u32[]{:S(2)}, u32[]{:S(2)}) collective-permute-start(bf16[1,15,256]{2,1,0:T(8,128)(2,1)S(1)} %get-tuple-element.199), channel_id=1, source_target_pairs={{4,0},{8,4},{12,8},{5,1},{9,5},{13,9},{6,2},{10,6},{14,10},{7,3},{... | collective-permute-start | bytes 23048 | tf_op jit(solution)/shard_map/ppermute | solution.py:18
  125.6 2.0 %copy-start.2 = (bf16[1,1792,256]{2,1,0:T(8,128)(2,1)S(1)}, bf16[1,1792,256]{2,1,0:T(8,128)(2,1)}, u32[]{:S(2)}) copy-start(bf16[1,1792,256]{2,1,0:T(8,128)(2,1)} %param.13) | copy-start | bytes 2752516
  125.6 2.0 %copy-start.9 = (pred[1792]{0:T(1024)(128)(4,1)S(1)}, pred[1792]{0:T(1024)(128)(4,1)}, u32[]{:S(2)}) copy-start(pred[1792]{0:T(1024)(128)(4,1)} %copy-done.8) | copy-start | bytes 5380
  125.6 2.0 %copy-start.11 = (f32[256]{0:T(256)S(1)}, f32[256]{0:T(256)}, u32[]{:S(2)}) copy-start(f32[256]{0:T(256)} %param.23) | copy-start | bytes 3076
Sparse Core Ops, SparseCore 0:
  17.0 43.9 all-gather.3
  91.2 6.6 reduce-scatter.2
  115.2 7.8 reduce-scatter.4
where the time goes:
time: 136 us; the launch traced here: 135 us
  waiting for transfers between devices  59 us (43%)
  matrix products  29.4 us (22%)
  between operations  14.1 us (10%)
  other arithmetic  12.3 us (9%)
  local copies, waits for them, and re-layouts  11 us (8%)
  starting transfers between devices  4.96 us (4%)
  blocking collectives  4.64 us (3%)
    all_gather x1, waiting for transfers between devices, shards(): segment = lax.all_gather(full_rows, 'tm', axis=1, tiled=True)  41.9 us
    dot_general x2, matrix products, merge_block(): jnp.einsum('rhqk,rhvk->rhqv', expo.astype(jnp.bfloat16), value_rows, pref...  10.1 us
    dot_general x2, matrix products, merge_block(): jnp.einsum('rqhd,rhdk->rhqk', query_set, key_rows, preferred_element_type...  9.57 us
    reduce_scatter x1, waiting for transfers between devices, shards(): lax.psum_scatter(conv_part.astype(jnp.bfloat16), 'head', scatter_dimensio...  8.03 us
    reduce_scatter x1, waiting for transfers between devices, shards(): lax.psum_scatter(partial_value.astype(jnp.bfloat16), 'head', scatter_dime...  5.76 us
    dot_general x1, matrix products, shards(): jnp.einsum('rsc,cd->rsd', hidden, conv_out, preferred_element_type=jnp.fl...  3.97 us
    reduce_sum x2, other arithmetic, merge_block(): denominator = denominator * factor + jnp.sum(expo, axis=-1)  3.65 us
    ppermute x1, starting transfers between devices, with_halo(): lax.ppermute(lax.slice_in_dim(block, block.shape[dim] - width, None, axis...  3.59 us
  transfers between devices with their start and end apart: 5, of which 4 were waited for; matrix products, arithmetic and copies ran while one was open for 3% of the time, Pallas kernels for 0%

commit v1 on v0

--- a/solution.py
+++ b/solution.py
@@ -5,6 +5,24 @@
 
 QDIM = 32
 VDIM = 12
+
+
+def ring_gather(value, axis, dim):
+    ways, here, step = (lax.axis_size(axis), lax.axis_index(axis), value.shape[dim])
+    dims = [n * ways if d == dim else n for d, n in enumerate(value.shape)]
+    full = lax.dynamic_update_slice_in_dim(
+        jnp.zeros(dims, value.dtype), value, here * step, axis=dim
+    )
+    going_up = going_down = value
+    for far in range(1, ways // 2 + 1):
+        going_up = lax.ppermute(going_up, axis, [(d, (d + 1) % ways) for d in range(ways)])
+        full = lax.dynamic_update_slice_in_dim(full, going_up, (here - far) % ways * step, axis=dim)
+        if 2 * far < ways:
+            going_down = lax.ppermute(going_down, axis, [(d, (d - 1) % ways) for d in range(ways)])
+            full = lax.dynamic_update_slice_in_dim(
+                full, going_down, (here + far) % ways * step, axis=dim
+            )
+    return full
 
 
 def with_halo(block, sides, width):
@@ -49,7 +67,7 @@
     heads_here = w_query.shape[1] // QDIM
     queries = jnp.einsum("rsd,dk->rsk", full_rows, w_query, preferred_element_type=jnp.float32)
     queries = queries.astype(jnp.bfloat16).reshape(records, quarter, heads_here, QDIM)
-    segment = lax.all_gather(full_rows, "tm", axis=1, tiled=True)
+    segment = ring_gather(full_rows, "tm", 1)
     keys_t = jnp.einsum("rnd,dk->rkn", segment, w_key, preferred_element_type=jnp.float32)
     values_t = jnp.einsum("rnd,dk->rkn", segment, w_value, preferred_element_type=jnp.float32)
     packed = jnp.concatenate([keys_t, values_t], axis=1).astype(jnp.bfloat16)

time: 136 us -> 126 us (0.926)
  waiting for transfers between devices: 59 us -> 46.5 us
  starting transfers between devices: 4.96 us -> 10.1 us
  matrix products: 29.4 us -> 26.7 us
    all_gather x1 -> x0, waiting for transfers between devices: 41.9 us -> none  [shards(): segment = lax.all_gather(full_rows, 'tm', axis=1, tiled=True)]
    ppermute x0 -> x3, waiting for transfers between devices: none -> 29.1 us  [the longest x2 20.4 us: ring_gather(): lax.ppermute(going_up, axis, [(d, (d + 1) % ways) for d in range(ways)])]
    ppermute x0 -> x3, starting transfers between devices: none -> 4.97 us  [the longest x2 2.94 us: ring_gather(): lax.ppermute(going_up, axis, [(d, (d + 1) % ways) for d in range(ways)])]
    dot_general x1, matrix products: 2.36 us -> 0.73 us  [shards(): jnp.einsum('rnd,dk->rkn', segment, w_key, preferred_element_type=jnp.floa...]
  transfers between devices with their start and end apart: 5 -> 7, of which waited for: 4 -> 6; matrix products, arithmetic and copies ran while one was open for 3% -> 3% of each run, Pallas kernels for 0% -> 0%
where the time goes in v1:
time: 126 us; the launch traced here: 125 us
  waiting for transfers between devices  46.5 us (37%)
  matrix products  26.7 us (21%)
  between operations  14.5 us (12%)
  other arithmetic  12.3 us (10%)
  local copies, waits for them, and re-layouts  10.5 us (8%)
  starting transfers between devices  10.1 us (8%)
  blocking collectives  4.52 us (4%)
    ppermute x2, waiting for transfers between devices, ring_gather(): lax.ppermute(going_up, axis, [(d, (d + 1) % ways) for d in range(ways)])  20.4 us
    dot_general x2, matrix products, merge_block(): jnp.einsum('rhqk,rhvk->rhqv', expo.astype(jnp.bfloat16), value_rows, pref...  10.1 us
    dot_general x2, matrix products, merge_block(): jnp.einsum('rqhd,rhdk->rhqk', query_set, key_rows, preferred_element_type...  9.58 us
    ppermute x1, waiting for transfers between devices, ring_gather(): lax.ppermute(going_down, axis, [(d, (d - 1) % ways) for d in range(ways)])  8.63 us
    reduce_scatter x1, waiting for transfers between devices, shards(): lax.psum_scatter(conv_part.astype(jnp.bfloat16), 'head', scatter_dimensio...  8.03 us
    reduce_scatter x1, waiting for transfers between devices, shards(): lax.psum_scatter(partial_value.astype(jnp.bfloat16), 'head', scatter_dime...  6.29 us
    dot_general x1, matrix products, shards(): jnp.einsum('rsc,cd->rsd', hidden, conv_out, preferred_element_type=jnp.fl...  3.97 us
    reduce_sum x2, other arithmetic, merge_block(): denominator = denominator * factor + jnp.sum(expo, axis=-1)  3.65 us
  transfers between devices with their start and end apart: 7, of which 6 were waited for; matrix products, arithmetic and copies ran while one was open for 3% of the time, Pallas kernels for 0%

profile of v1, /device:TPU:0, one launch (start us, length us, event | category | flops | bytes accessed | tf_op | source)
XLA Modules:
  0.0 125.3 jit_solution(5516409879806169344)
XLA Ops:
  6.5 0.0 copy-start
  6.5 0.0 reduce-scatter.3.cloned.1.call-start
  7.3 0.0 copy-start.7
  7.3 0.6 copy-done.7
  7.8 2.7 %select_convert_fusion = f32[1,1792,256]{2,1,0:T(8,128)} fusion(bf16[1,1792,256]{2,1,0:T(8,128)(2,1)} %param.13, pred[1792]{0:T(1024)(128)(4,1)S(1)} %add_compare_fusion), kind=kLoop, calls=%fused_computation.72 | loop fusion | flops 917504 | bytes 2754304 | tf_op jit(solution)/shard_map/convert_element_type | solution.py:61
  10.6 1.8 %reshape.462 = f32[1,448,4,256]{3,2,1,0:T(4,128)S(1)} reshape(f32[1,1792,256]{2,1,0:T(8,128)} %select_convert_fusion) | data formatting | bytes 3670016 | tf_op jit(solution)/shard_map/convert_element_type | solution.py:61
  12.4 0.0 copy-done.9
  12.5 0.0 copy-start.4
  12.5 1.3 %multiply_reduce_fusion = bf16[448,256]{1,0:T(8,128)(2,1)S(1)} fusion(f32[1,448,4,256]{3,2,1,0:T(4,128)S(1)} %reshape.462, f32[4,256]{1,0:T(4,128)S(1)} %copy-done.9), kind=kLoop, calls=%fused_computation.37 | loop fusion | flops 802816 | bytes 2068480 | tf_op jit(solution)/shard_map/reduce_sum | solution.py:62
  13.8 0.0 copy-start.2
  13.8 2.3 %all-gather = bf16[448,512]{1,0:T(8,128)(2,1)S(1)} all-gather(bf16[448,256]{1,0:T(8,128)(2,1)S(1)} %multiply_reduce_fusion), channel_id=2, replica_groups=mesh['groups'=2,'tm'=4,'dp'=2,'head'=2] {'head'}, dimensions={1}, use_global_device_ids=true | all-gather | bytes 688128 | tf_op jit(solution)/shard_map/all_gather | solution.py:66
  16.0 0.0 copy-done.2
  16.0 2.9 %collective-permute-start = (bf16[1,448,512]{2,1,0:T(8,128)(2,1)S(1)}, bf16[1,448,512]{2,1,0:T(8,128)(2,1)S(1)}, u32[]{:S(2)}, u32[]{:S(2)}) collective-permute-start(bf16[1,448,512]{2,1,0:T(8,128)(2,1)S(1)} %bitcast.152), channel_id=1, source_target_pairs={{0,4},{4,8},{8,12},{12,0},{1,5},{5,9},{9,13},{13,1},{2,6},{6,10},{... | collective-permute-start | bytes 1376264 | tf_op jit(solution)/shard_map/ppermute | solution.py:18
  19.0 2.0 %collective-permute-start.1 = (bf16[1,448,512]{2,1,0:T(8,128)(2,1)S(1)}, bf16[1,448,512]{2,1,0:T(8,128)(2,1)S(1)}, u32[]{:S(2)}, u32[]{:S(2)}) collective-permute-start(bf16[1,448,512]{2,1,0:T(8,128)(2,1)S(1)} %bitcast.153), channel_id=1, source_target_pairs={{0,12},{4,0},{8,4},{12,8},{1,13},{5,1},{9,5},{13,9},{2,14},{6,2},{... | collective-permute-start | bytes 1376264 | tf_op jit(solution)/shard_map/ppermute | solution.py:21
  21.0 0.0 copy-done.4
  21.0 0.3 convolution_convert_fusion.4
  21.4 0.8 copy.14
  22.2 0.1 broadcast.232
  22.3 0.0 copy-start.3
  22.4 10.1 %collective-permute-done = bf16[1,448,512]{2,1,0:T(8,128)(2,1)S(1)} collective-permute-done((bf16[1,448,512]{2,1,0:T(8,128)(2,1)S(1)}, bf16[1,448,512]{2,1,0:T(8,128)(2,1)S(1)}, u32[]{:S(2)}, u32[]{:S(2)}) %collective-permute-start) | collective-permute-done | bytes 458784 | tf_op jit(solution)/shard_map/ppermute | solution.py:18
  32.4 0.0 collective-permute-start.2
  32.5 8.6 %collective-permute-done.1 = bf16[1,448,512]{2,1,0:T(8,128)(2,1)S(1)} collective-permute-done((bf16[1,448,512]{2,1,0:T(8,128)(2,1)S(1)}, bf16[1,448,512]{2,1,0:T(8,128)(2,1)S(1)}, u32[]{:S(2)}, u32[]{:S(2)}) %collective-permute-start.1) | collective-permute-done | bytes 458784 | tf_op jit(solution)/shard_map/ppermute | solution.py:21
  41.1 0.0 copy-start.6
  41.1 10.4 %collective-permute-done.2 = bf16[1,448,512]{2,1,0:T(8,128)(2,1)S(1)} collective-permute-done((bf16[1,448,512]{2,1,0:T(8,128)(2,1)S(1)}, bf16[1,448,512]{2,1,0:T(8,128)(2,1)S(1)}, u32[]{:S(2)}, u32[]{:S(2)}) %collective-permute-start.2) | collective-permute-done | bytes 458784 | tf_op jit(solution)/shard_map/ppermute | solution.py:18
  51.6 0.0 copy-done.3
  51.6 0.7 fusion.23
  52.3 0.0 copy-done.6
  52.3 0.6 fusion.24
  53.0 0.0 copy-start.5
  53.0 25.0 %while.18 = (s32[]{:T(128)}, f32[1,4,448]{2,1,0:T(4,128)S(1)}, f32[1,4,448]{2,1,0:T(4,128)S(1)}, f32[1,4,448,12]{2,3,1,0:T(8,128)}, s32[1]{0:T(128)}, /*index=5*...) while((s32[]{:T(128)}, f32[1,4,448]{2,1,0:T(4,128)S(1)}, ...), condition=%wide.region_4.5_spmd.clone, body=%wide.region_1.4_spmd.clone.sunk | while | flops 162245888 | bytes 40058620 | solution.py:115
  53.1 4.8 %bitcast_reduce_fusion.2 = (f32[4,448]{1,0:T(4,128)S(1)}, f32[4,896,448]{1,2,0:T(8,128)}) fusion(pred[896]{0:T(1024)(128)(4,1)S(1)} %fusion.96, bf16[4,32,896]{2,1,0:T(8,128)(2,1)S(1)} %bitcast.151, bf16[1,448,4,32]{1,3,2,0:T(8,128)(2,1)} %get-tuple-element.312), kind=kOutput, calls=%fused_computation.2.clone.1 | convolution fusion | flops 107575552 | bytes 6774656 | tf_op jit(solution)/shard_map/while/body/eval_jaxpr/rqhd,rhdk->rhqk/dot_general | solution.py:91
  57.9 0.0 slice-start
  57.9 0.7 reshape.472
  58.6 5.0 %fusion.99 = f32[1,4,448,12]{2,3,1,0:T(8,128)} fusion(bf16[4,12,896]{2,1,0:T(8,128)(2,1)} %reshape.472, f32[4,896,448]{1,2,0:T(8,128)} %get-tuple-element.280, f32[4,448]{1,0:T(4,128)S(1)} %bitcast.154, pred[896]{0:T(1024)(128)(4,1)S(1)} %fusion.96, f32[1,4,448,12]{2,3,1,0:T(8,128)} %get-tuple-element.297, f32[4,448]{1,0:T(4,128)S(1)} %get-tuple-element.281, ...), kind=kOutput, calls=%fused_computation.12.clone.1 | convolution fusion | flops 46627840 | bytes 6695809 | tf_op jit(solution)/shard_map/while/body/eval_jaxpr/rhqk,rhvk->rhqv/dot_general | solution.py:101
  63.6 0.0 slice-done.1
  63.6 1.8 %fusion.98 = f32[4,448]{1,0:T(4,128)S(1)} fusion(f32[4,896,448]{1,2,0:T(8,128)S(1)} %bitcast.150, f32[4,448]{1,0:T(4,128)S(1)} %bitcast.155, pred[896]{0:T(1024)(128)(4,1)S(1)} %fusion.96), kind=kLoop, calls=%fused_computation.7.clone.1 | loop fusion | flops 8026368 | bytes 6437760 | tf_op jit(solution)/shard_map/while/body/eval_jaxpr/reduce_sum | solution.py:100
  65.6 4.8 %bitcast_reduce_fusion.2 = (f32[4,448]{1,0:T(4,128)S(1)}, f32[4,896,448]{1,2,0:T(8,128)}) fusion(pred[896]{0:T(1024)(128)(4,1)S(1)} %fusion.96, bf16[4,32,896]{2,1,0:T(8,128)(2,1)S(1)} %bitcast.151, bf16[1,448,4,32]{1,3,2,0:T(8,128)(2,1)} %get-tuple-element.312), kind=kOutput, calls=%fused_computation.2.clone.1 | convolution fusion | flops 107575552 | bytes 6774656 | tf_op jit(solution)/shard_map/while/body/eval_jaxpr/rqhd,rhdk->rhqk/dot_general | solution.py:91
  70.4 0.0 slice-start
  70.4 0.7 reshape.472
  71.1 5.0 %fusion.99 = f32[1,4,448,12]{2,3,1,0:T(8,128)} fusion(bf16[4,12,896]{2,1,0:T(8,128)(2,1)} %reshape.472, f32[4,896,448]{1,2,0:T(8,128)} %get-tuple-element.280, f32[4,448]{1,0:T(4,128)S(1)} %bitcast.154, pred[896]{0:T(1024)(128)(4,1)S(1)} %fusion.96, f32[1,4,448,12]{2,3,1,0:T(8,128)} %get-tuple-element.297, f32[4,448]{1,0:T(4,128)S(1)} %get-tuple-element.281, ...), kind=kOutput, calls=%fused_computation.12.clone.1 | convolution fusion | flops 46627840 | bytes 6695809 | tf_op jit(solution)/shard_map/while/body/eval_jaxpr/rhqk,rhvk->rhqv/dot_general | solution.py:101
  76.1 1.8 %fusion.98 = f32[4,448]{1,0:T(4,128)S(1)} fusion(f32[4,896,448]{1,2,0:T(8,128)S(1)} %bitcast.150, f32[4,448]{1,0:T(4,128)S(1)} %bitcast.155, pred[896]{0:T(1024)(128)(4,1)S(1)} %fusion.96), kind=kLoop, calls=%fused_computation.7.clone.1 | loop fusion | flops 8026368 | bytes 6437760 | tf_op jit(solution)/shard_map/while/body/eval_jaxpr/reduce_sum | solution.py:100
  78.0 0.9 fusion.69
  79.0 1.1 fusion.28
  80.0 0.0 reduce-scatter.3.cloned.1.call-update
  80.1 0.0 reduce-scatter.5.cloned.1.call-start
  80.1 1.0 fusion.73
  81.2 6.3 %reduce-scatter.3.cloned.1.call-done = bf16[1,448,256]{2,1,0:T(8,128)(2,1)} async-done(((bf16[1,448,512]{2,1,0:T(8,128)(2,1)}), bf16[1,448,256]{2,1,0:T(8,128)(2,1)}) %reduce-scatter.3.cloned.1.call-update) | async-done | bytes 229392 | tf_op jit(solution)/shard_map/reduce_scatter | solution.py:123
  87.4 1.1 fusion.37
  88.5 0.0 copy-start.11
  88.6 2.3 %all_gather.7 = bf16[1,448,512]{2,1,0:T(8,128)(2,1)S(1)} all-gather(bf16[1,448,256]{2,1,0:T(8,128)(2,1)S(1)} %fusion.37), channel_id=1, replica_groups=mesh['groups'=2,'tm'=4,'dp'=2,'head'=2] {'head'}, dimensions={2}, use_global_device_ids=true | all-gather | bytes 688128 | tf_op jit(solution)/shard_map/all_gather | solution.py:127
  90.8 0.4 convolution_bitcast_fusion
  91.2 0.2 fusion.39
  91.4 3.6 %collective-permute-start.3 = (bf16[1,15,256]{2,1,0:T(8,128)(2,1)S(1)}, bf16[1,15,256]{2,1,0:T(8,128)(2,1)S(1)}, u32[]{:S(2)}, u32[]{:S(2)}) collective-permute-start(bf16[1,15,256]{2,1,0:T(8,128)(2,1)S(1)} %get-tuple-element.198), channel_id=1, source_target_pairs={{0,4},{4,8},{8,12},{1,5},{5,9},{9,13},{2,6},{6,10},{10,14},{3,7},{... | collective-permute-start | bytes 23048 | tf_op jit(solution)/shard_map/ppermute | solution.py:33
  95.0 1.5 %collective-permute-start.4 = (bf16[1,15,256]{2,1,0:T(8,128)(2,1)S(1)}, bf16[1,15,256]{2,1,0:T(8,128)(2,1)S(1)}, u32[]{:S(2)}, u32[]{:S(2)}) collective-permute-start(bf16[1,15,256]{2,1,0:T(8,128)(2,1)S(1)} %get-tuple-element.199), channel_id=1, source_target_pairs={{4,0},{8,4},{12,8},{5,1},{9,5},{13,9},{6,2},{10,6},{14,10},{7,3},{... | collective-permute-start | bytes 23048 | tf_op jit(solution)/shard_map/ppermute | solution.py:36
  96.5 1.0 fusion.74
  97.5 0.0 collective-permute-done.3
  97.5 3.1 %collective-permute-done.4 = bf16[1,15,256]{2,1,0:T(8,128)(2,1)S(1)} collective-permute-done((bf16[1,15,256]{2,1,0:T(8,128)(2,1)S(1)}, bf16[1,15,256]{2,1,0:T(8,128)(2,1)S(1)}, u32[]{:S(2)}, u32[]{:S(2)}) %collective-permute-start.4) | collective-permute-done | bytes 7712 | tf_op jit(solution)/shard_map/ppermute | solution.py:36
  100.5 4.0 %fusion.29 = bf16[1,448,512]{2,1,0:T(8,128)(2,1)} fusion(bf16[256,512]{1,0:T(8,128)(2,1)S(1)} %copy-done.11, bf16[1,448,256]{2,1,0:T(8,128)(2,1)S(1)} %fusion.39, bf16[1,15,256]{2,1,0:T(8,128)(2,1)S(1)} %collective-permute-done.4, bf16[1,15,256]{2,1,0:T(8,128)(2,1)S(1)} %collective-permute-done.3, f32[256]{0:T(256)S(1)} %bitcast.186, f32[256]{0:T(256)S(1)} %bitcast.187, ...), kind=kOutput, calls=%fused_computation.70 | convolution fusion | flops 139116544 | bytes 997376 | tf_op jit(solution)/shard_map/rsc,cd->rsd/dot_general | solution.py:139
  104.5 0.0 reduce-scatter.5.cloned.1.call-update
  104.5 8.0 %reduce-scatter.5.cloned.1.call-done = bf16[1,448,256]{2,1,0:T(8,128)(2,1)} async-done(((bf16[1,448,512]{2,1,0:T(8,128)(2,1)}), bf16[1,448,256]{2,1,0:T(8,128)(2,1)}) %reduce-scatter.5.cloned.1.call-update) | async-done | bytes 229392 | tf_op jit(solution)/shard_map/reduce_scatter | solution.py:140
  112.6 1.0 add_bitcast_fusion
  113.6 1.6 %broadcast_in_dim.111 = f32[448,4,256]{2,1,0:T(4,128)} broadcast(f32[448,256]{1,0:T(8,128)S(1)} %add_bitcast_fusion), dimensions={0,2} | broadcast | bytes 2293760 | tf_op jit(solution)/shard_map/broadcast_in_dim | solution.py:144
  115.1 2.0 %broadcast_in_dim.112 = f32[1,1792,256]{2,1,0:T(8,128)S(1)} reshape(f32[448,4,256]{2,1,0:T(4,128)} %broadcast_in_dim.111) | data formatting | bytes 3670016 | tf_op jit(solution)/shard_map/broadcast_in_dim | solution.py:144
  117.2 1.3 %fusion.27 = bf16[1,1792,256]{2,1,0:T(8,128)(2,1)} fusion(f32[1,1792,256]{2,1,0:T(8,128)S(1)} %broadcast_in_dim.112, bf16[1,1792,256]{2,1,0:T(8,128)(2,1)S(1)} %copy-done.1, f32[256]{0:T(256)S(1)} %copy-done.10, pred[1792]{0:T(1024)(128)(4,1)S(1)} %copy-done.8), kind=kLoop, calls=%fused_computation.36 | loop fusion | flops 2752512 | bytes 3672832 | tf_op jit(solution)/shard_map/convert_element_type | solution.py:147
  (41 shorter events, 0.5 us)
Async XLA Ops:
  6.5 84.3 %copy-start = (bf16[512,2,256]{2,1,0:T(2,128)(2,1)S(1)}, bf16[512,2,256]{2,1,0:T(2,128)(2,1)}, u32[]{:S(2)}) copy-start(bf16[512,2,256]{2,1,0:T(2,128)(2,1)} %param.20) | copy-start | bytes 1572868
  6.5 80.9 %reduce-scatter.3.cloned.1.call-start = ((), (), s32[]{:S(2)}) async-start(), calls=%async_computation.2 | async-start | bytes 688128 | tf_op jit(solution)/shard_map/reduce_scatter | solution.py:123
  7.3 0.6 copy-start.7
  10.6 1.9 %copy-start.9 = (f32[4,256]{1,0:T(4,128)S(1)}, f32[4,256]{1,0:T(4,128)}, u32[]{:S(2)}) copy-start(f32[4,256]{1,0:T(4,128)} %param.15) | copy-start | bytes 12292
  12.5 8.6 %copy-start.4 = (bf16[512,128]{1,0:T(8,128)(2,1)S(1)}, bf16[512,128]{1,0:T(8,128)(2,1)}, u32[]{:S(2)}) copy-start(bf16[512,128]{1,0:T(8,128)(2,1)} %param.16) | copy-start | bytes 393220
  13.8 2.3 %copy-start.2 = (bf16[448,256]{1,0:T(8,128)(2,1)}, bf16[448,256]{1,0:T(8,128)(2,1)S(1)}, u32[]{:S(2)}) copy-start(bf16[448,256]{1,0:T(8,128)(2,1)S(1)} %multiply_reduce_fusion) | copy-start | bytes 688132
  16.0 16.4 %collective-permute-start = (bf16[1,448,512]{2,1,0:T(8,128)(2,1)S(1)}, bf16[1,448,512]{2,1,0:T(8,128)(2,1)S(1)}, u32[]{:S(2)}, u32[]{:S(2)}) collective-permute-start(bf16[1,448,512]{2,1,0:T(8,128)(2,1)S(1)} %bitcast.152), channel_id=1, source_target_pairs={{0,4},{4,8},{8,12},{12,0},{1,5},{5,9},{9,13},{13,1},{2,6},{6,10},{... | collective-permute-start | bytes 1376264 | tf_op jit(solution)/shard_map/ppermute | solution.py:18
  19.0 22.1 %collective-permute-start.1 = (bf16[1,448,512]{2,1,0:T(8,128)(2,1)S(1)}, bf16[1,448,512]{2,1,0:T(8,128)(2,1)S(1)}, u32[]{:S(2)}, u32[]{:S(2)}) collective-permute-start(bf16[1,448,512]{2,1,0:T(8,128)(2,1)S(1)} %bitcast.153), channel_id=1, source_target_pairs={{0,12},{4,0},{8,4},{12,8},{1,13},{5,1},{9,5},{13,9},{2,14},{6,2},{... | collective-permute-start | bytes 1376264 | tf_op jit(solution)/shard_map/ppermute | solution.py:21
  22.3 29.3 %copy-start.3 = (bf16[512,128]{1,0:T(8,128)(2,1)S(1)}, bf16[512,128]{1,0:T(8,128)(2,1)}, u32[]{:S(2)}) copy-start(bf16[512,128]{1,0:T(8,128)(2,1)} %param.17) | copy-start | bytes 393220
  32.4 19.1 %collective-permute-start.2 = (bf16[1,448,512]{2,1,0:T(8,128)(2,1)S(1)}, bf16[1,448,512]{2,1,0:T(8,128)(2,1)S(1)}, u32[]{:S(2)}, u32[]{:S(2)}) collective-permute-start(bf16[1,448,512]{2,1,0:T(8,128)(2,1)S(1)} %collective-permute-done), channel_id=1, source_target_pairs={{0,4},{4,8},{8,12},{12,0},{1,5},{5,9},{9,13},{13,1},{2,6},{6,10},{... | collective-permute-start | bytes 1376264 | tf_op jit(solution)/shard_map/ppermute | solution.py:18
  41.1 11.2 %copy-start.6 = (bf16[512,48]{0,1:T(8,128)(2,1)S(1)}, bf16[512,48]{0,1:T(8,128)(2,1)}, u32[]{:S(2)}) copy-start(bf16[512,48]{0,1:T(8,128)(2,1)} %param.18) | copy-start | bytes 147460
  53.0 25.9 %copy-start.5 = (bf16[48,512]{1,0:T(8,128)(2,1)S(1)}, bf16[48,512]{1,0:T(8,128)(2,1)}, u32[]{:S(2)}) copy-start(bf16[48,512]{1,0:T(8,128)(2,1)} %param.19) | copy-start | bytes 147460
  57.9 5.7 %slice-start = ((s8[6422528]{0:T(1024)(128)(4,1)}), s8[2228224]{0:T(1024)(128)(4,1)S(1)}, s32[]{:S(2)}) async-start(s8[6422528]{0:T(1024)(128)(4,1)} %bitcast.149), calls=%async_computation.4 | async-start | bytes 4456448 | tf_op jit(solution)/shard_map/while
  58.6 5.0 %slice-start.1 = ((s8[6422528]{0:T(1024)(128)(4,1)}), s8[4194304]{0:T(1024)(128)(4,1)S(1)}, s32[]{:S(2)}) async-start(s8[6422528]{0:T(1024)(128)(4,1)} %bitcast.149), calls=%async_computation.5 | async-start | bytes 8388608 | tf_op jit(solution)/shard_map/while
  70.4 5.7 %slice-start = ((s8[6422528]{0:T(1024)(128)(4,1)}), s8[2228224]{0:T(1024)(128)(4,1)S(1)}, s32[]{:S(2)}) async-start(s8[6422528]{0:T(1024)(128)(4,1)} %bitcast.149), calls=%async_computation.4 | async-start | bytes 4456448 | tf_op jit(solution)/shard_map/while
  71.1 5.0 %slice-start.1 = ((s8[6422528]{0:T(1024)(128)(4,1)}), s8[4194304]{0:T(1024)(128)(4,1)S(1)}, s32[]{:S(2)}) async-start(s8[6422528]{0:T(1024)(128)(4,1)} %bitcast.149), calls=%async_computation.5 | async-start | bytes 8388608 | tf_op jit(solution)/shard_map/while
  80.1 32.5 %reduce-scatter.5.cloned.1.call-start = ((), (), s32[]{:S(2)}) async-start(), calls=%async_computation.3 | async-start | bytes 688128 | tf_op jit(solution)/shard_map/reduce_scatter | solution.py:140
  88.5 12.0 %copy-start.11 = (bf16[256,512]{1,0:T(8,128)(2,1)S(1)}, bf16[256,512]{1,0:T(8,128)(2,1)}, u32[]{:S(2)}) copy-start(bf16[256,512]{1,0:T(8,128)(2,1)} %param.22) | copy-start | bytes 786436
  91.4 6.1 %collective-permute-start.3 = (bf16[1,15,256]{2,1,0:T(8,128)(2,1)S(1)}, bf16[1,15,256]{2,1,0:T(8,128)(2,1)S(1)}, u32[]{:S(2)}, u32[]{:S(2)}) collective-permute-start(bf16[1,15,256]{2,1,0:T(8,128)(2,1)S(1)} %get-tuple-element.198), channel_id=1, source_target_pairs={{0,4},{4,8},{8,12},{1,5},{5,9},{9,13},{2,6},{6,10},{10,14},{3,7},{... | collective-permute-start | bytes 23048 | tf_op jit(solution)/shard_map/ppermute | solution.py:33
  95.0 5.5 %collective-permute-start.4 = (bf16[1,15,256]{2,1,0:T(8,128)(2,1)S(1)}, bf16[1,15,256]{2,1,0:T(8,128)(2,1)S(1)}, u32[]{:S(2)}, u32[]{:S(2)}) collective-permute-start(bf16[1,15,256]{2,1,0:T(8,128)(2,1)S(1)} %get-tuple-element.199), channel_id=1, source_target_pairs={{4,0},{8,4},{12,8},{5,1},{9,5},{13,9},{6,2},{10,6},{14,10},{7,3},{... | collective-permute-start | bytes 23048 | tf_op jit(solution)/shard_map/ppermute | solution.py:36
  115.1 2.0 %copy-start.1 = (bf16[1,1792,256]{2,1,0:T(8,128)(2,1)S(1)}, bf16[1,1792,256]{2,1,0:T(8,128)(2,1)}, u32[]{:S(2)}) copy-start(bf16[1,1792,256]{2,1,0:T(8,128)(2,1)} %param.13) | copy-start | bytes 2752516
  115.1 2.0 %copy-start.8 = (pred[1792]{0:T(1024)(128)(4,1)S(1)}, pred[1792]{0:T(1024)(128)(4,1)}, u32[]{:S(2)}) copy-start(pred[1792]{0:T(1024)(128)(4,1)} %copy-done.7) | copy-start | bytes 5380
  115.1 2.0 %copy-start.10 = (f32[256]{0:T(256)S(1)}, f32[256]{0:T(256)}, u32[]{:S(2)}) copy-start(f32[256]{0:T(256)} %param.23) | copy-start | bytes 3076
Sparse Core Ops, SparseCore 0:
  80.2 7.2 reduce-scatter.2
  104.7 7.8 reduce-scatter.4
